TPU v7x, 128 devices: a whole 4x4x4 slice. The times are simulated.
128 devices in a mesh: grp: 2 (over core), ctx: 64 (over y, x, z).
Axes of the slice: x: 4, y: 4, z: 4, core: 2. Of those that a mesh axis runs over, the one named last changes fastest.
Arguments:
- queries: bfloat16 [98304, 32, 128], P(('grp', 'ctx')), may hold values from -6 to 6
- keys: bfloat16 [98304, 32, 128], P(('grp', 'ctx')), may hold values from -6 to 6
- values: bfloat16 [98304, 32, 128], P(('grp', 'ctx')), may hold values from -6 to 6
- norm_gain: float32 [4096], replicated, may hold values from 0.5 to 1.5
Outputs:
- attended: bfloat16 [98304, 32, 128], P(('grp', 'ctx'))
All inputs are finite; a program needn't handle non-finite values.
Results may differ from a plain program's by a relative error of at most 0.0049.
Values sent between devices are 32-bit elements; how exact they have to be, the bound alone decides.
No kernel may reach another device: no remote copies, remote signals or barrier semaphores. Data moves between devices by JAX's collectives and lax.ppermute only.
A program may use at most 640 MiB of HBM per device.

v0:
```python
import jax
import jax.numpy as jnp
from jax import lax
from jax.sharding import PartitionSpec as P

BLOCK = 128


def carried_in(part, axis, combine, identity):
    place = lax.axis_index(axis)
    gathered = lax.all_gather(part, axis)
    state = jnp.zeros_like(part) + jnp.asarray(identity, part.dtype)

    def one(step, state):
        return combine(state, lax.dynamic_index_in_dim(gathered, step, 0, False))

    return lax.fori_loop(0, place, one, state)


def spread(value, axis, source):
    kept = jnp.where(lax.axis_index(axis) == source, value, 0).astype(value.dtype)
    return lax.psum(kept, axis)


def from_behind(block, axis, distance):
    devices = range(lax.axis_size(axis))
    route = [(i - distance, i) for i in devices if i - distance in devices]
    return lax.ppermute(block, axis, route)


def add_states(earlier, later):
    return earlier + later


def per_device(queries, keys, values, norm_gain):
    rows, heads, width = queries.shape
    count = rows // BLOCK
    qs = queries.reshape(count, BLOCK, heads, width)
    ks = keys.reshape(count, BLOCK, heads, width)
    vs = values.reshape(count, BLOCK, heads, width)
    pieces = jnp.einsum("ckhd,ckhe->chde", ks, vs, preferred_element_type=jnp.float32)
    total = jnp.sum(pieces, axis=0)
    local_before = jnp.cumsum(pieces, axis=0) - pieces
    empty = jnp.zeros_like(total)
    within = carried_in(total, "ctx", add_states, empty)
    group_sum = spread(within + total, "ctx", lax.axis_size("ctx") - 1)
    earlier = from_behind(group_sum, "grp", 1)
    prefix = earlier + within
    states = (prefix[None] + local_before).astype(jnp.bfloat16)
    inter = jnp.einsum("cqhd,chde->cqhe", qs, states, preferred_element_type=jnp.float32)
    scores = jnp.einsum("cqhd,ckhd->chqk", qs, ks, preferred_element_type=jnp.float32)
    position = jnp.arange(BLOCK)
    causal = position[:, None] >= position[None, :]
    scores = jnp.where(causal[None, None], scores, 0.0).astype(jnp.bfloat16)
    intra = jnp.einsum("chqk,ckhd->cqhd", scores, vs, preferred_element_type=jnp.float32)
    mixed = intra + inter
    power = jnp.mean(mixed * mixed, axis=(2, 3), keepdims=True)
    gain = norm_gain.reshape(heads, width)
    normed = mixed * lax.rsqrt(power + 1e-06) * gain[None, None]
    return normed.astype(jnp.bfloat16).reshape(rows, heads, width)


def solution(mesh):
    in_specs = (
        P(("grp", "ctx"), None, None),
        P(("grp", "ctx"), None, None),
        P(("grp", "ctx"), None, None),
        P(),
    )
    out_specs = P(("grp", "ctx"), None, None)
    return jax.shard_map(
        per_device, mesh=mesh, in_specs=in_specs, out_specs=out_specs, check_vma=False
    )
```

profile of v0, /device:TPU:0, one launch (start us, length us, event | category | flops | bytes accessed | tf_op | source)
XLA Modules:
  0.0 888.8 jit_solution(6899667623402443073)
XLA Ops:
  6.5 0.0 all-gather.3.cloned.1.call-start
  6.5 9.1 %copy.17 = bf16[6,128,32,128]{1,3,2,0:T(8,128)(2,1)} copy(bf16[6,128,32,128]{3,2,1,0:T(8,128)(2,1)} %bitcast.33) | data formatting | bytes 12582912 | tf_op jit(solution)/shard_map/reshape | solution.py:39
  15.6 15.0 %fusion.12 = (f32[32,128,128]{2,1,0:T(8,128)}, f32[6,32,128,128]{3,2,1,0:T(8,128)}) fusion(bf16[6,128,32,128]{1,3,2,0:T(8,128)(2,1)} %copy.17, bf16[6,128,32,128]{3,2,1,0:T(8,128)(2,1)} %bitcast.29), kind=kOutput, calls=%fused_computation.21 | convolution fusion | flops 807927808 | bytes 27262976 | tf_op jit(solution)/shard_map/ckhd,ckhe->chde/dot_general | solution.py:41
  30.7 0.0 all-gather.3.cloned.1.call-update
  30.7 0.0 all-reduce.2.cloned.1.call-start
  30.7 515.4 %all-gather.3.cloned.1.call-done = f32[2048,128,128]{2,1,0:T(8,128)} async-done(((f32[32,128,128]{2,1,0:T(8,128)}), f32[2048,128,128]{2,1,0:T(8,128)}) %all-gather.3.cloned.1.call-update) | async-done | bytes 134217744 | tf_op jit(solution)/shard_map/all_gather | solution.py:11
  546.1 0.2 broadcast_in_dim.24
  546.4 3.2 add_select_fusion
  549.6 0.0 all-reduce.2.cloned.1.call-update
  549.7 267.4 %all-reduce.2.cloned.1.call-done = f32[32,128,128]{2,1,0:T(8,128)} async-done(((f32[32,128,128]{2,1,0:T(8,128)}), f32[32,128,128]{2,1,0:T(8,128)}) %all-reduce.2.cloned.1.call-update) | async-done | bytes 2097168 | tf_op jit(solution)/shard_map/psum | solution.py:22
  817.1 2.6 collective-permute-start
  819.6 8.4 fusion.13
  828.0 14.6 %fusion = f32[6,32,128,128]{3,2,1,0:T(8,128)} fusion(pred[128,128]{1,0:T(8,128)(4,1)S(1)} %iota_compare_fusion, bf16[6,128,32,128]{3,2,1,0:T(8,128)(2,1)} %bitcast.30, bf16[6,128,32,128]{1,3,2,0:T(8,128)(2,1)} %copy.17, bf16[6,128,32,128]{3,2,1,0:T(8,128)(2,1)} %bitcast.31), kind=kOutput, calls=%fused_computation.6 | convolution fusion | flops 1613758464 | bytes 31473664 | tf_op jit(solution)/shard_map/chqk,ckhd->cqhd/dot_general | solution.py:55
  842.7 0.0 collective-permute-done
  842.7 1.8 add.41
  844.5 0.0 copy-start
  844.5 21.0 %multiply_reduce_fusion = (f32[6,128]{1,0:T(8,128)S(1)}, f32[6,32,128,128]{2,3,1,0:T(8,128)}) fusion(f32[6,32,128,128]{3,2,1,0:T(8,128)} %fusion, f32[6,32,128,128]{3,2,1,0:T(8,128)} %fusion.13, f32[6,32,128,128]{3,2,1,0:T(8,128)} %get-tuple-element.38, f32[32,128,128]{2,1,0:T(8,128)S(1)} %add.41, bf16[6,128,32,128]{3,2,1,0:T(8,128)(2,1)} %bitcast.32), kind=kOutput, calls=%fused_computation.3 | convolution fusion | flops 824179968 | bytes 58723328 | tf_op jit(solution)/shard_map/cqhd,chde->cqhe/dot_general | solution.py:50
  865.5 0.0 copy-done
  865.5 9.6 %multiply_convert_fusion = bf16[6,128,32,128]{3,1,2,0:T(8,128)(2,1)S(1)} fusion(f32[32,128]{1,0:T(8,128)S(1)} %bitcast.34, f32[6,128]{1,0:T(8,128)S(1)} %add_rsqrt_fusion, f32[6,32,128,128]{2,3,1,0:T(8,128)} %get-tuple-element.40, f32[6,32,128,128]{3,2,1,0:T(8,128)} %fusion), kind=kLoop, calls=%fused_computation.2 | loop fusion | flops 12582912 | bytes 31476736 | tf_op jit(solution)/shard_map/convert_element_type | solution.py:60
  875.2 6.8 copy.20
  (3 shorter events, 0.0 us)
Async XLA Ops:
  6.5 539.6 %all-gather.3.cloned.1.call-start = ((), (), s32[]{:S(2)}) async-start(), calls=%async_computation.1 | async-start | bytes 136314880 | tf_op jit(solution)/shard_map/all_gather | solution.py:11
  30.7 786.4 %all-reduce.2.cloned.1.call-start = ((), (), s32[]{:S(2)}) async-start(), calls=%async_computation | async-start | bytes 4194304 | tf_op jit(solution)/shard_map/psum | solution.py:22
  817.1 25.6 %collective-permute-start = (f32[32,128,128]{2,1,0:T(8,128)}, f32[32,128,128]{2,1,0:T(8,128)}, u32[]{:S(2)}, u32[]{:S(2)}) collective-permute-start(f32[32,128,128]{2,1,0:T(8,128)} %all-reduce.2.cloned.1.call-done), channel_id=1, source_target_pairs={{0,64},{1,65},{2,66},{3,67},{4,68},{5,69},{6,70},{7,71},{8,72},{9,... | collective-permute-start | bytes 6291464 | tf_op jit(solution)/shard_map/ppermute | solution.py:28
  844.5 21.0 %copy-start = (f32[4096]{0:T(1024)S(1)}, f32[4096]{0:T(1024)}, u32[]{:S(2)}) copy-start(f32[4096]{0:T(1024)} %param.9) | copy-start | bytes 49156
Sparse Core Ops, SparseCore 0:
  30.8 515.2 all-gather.2
  551.0 266.0 all-reduce.1
where the time goes:
time: 891 us; the launch traced here: 889 us
  waiting for transfers between devices  783 us (88%)
  matrix products  50.6 us (6%)
  other arithmetic  23.1 us (3%)
  local copies, waits for them, and re-layouts  16.1 us (2%)
  between operations  13.5 us (2%)
    all_gather x1, waiting for transfers between devices, carried_in(): gathered = lax.all_gather(part, axis)  515 us
    psum x1, waiting for transfers between devices, spread(): return lax.psum(kept, axis)  267 us
    dot_general x1, matrix products, per_device(): jnp.einsum('cqhd,chde->cqhe', qs, states, preferred_element_type=jnp.floa...  21 us
  transfers between devices with their start and end apart: 3, of which 2 were waited for; matrix products, arithmetic and copies ran while one was open for 3% of the time, Pallas kernels for 0%

commit v1 on v0

v1 whole, which is shorter than its diff:
```python
import jax
import jax.numpy as jnp
from jax import lax
from jax.experimental import pallas as pl
from jax.experimental.pallas import tpu as pltpu
from jax.sharding import PartitionSpec as P


HD = 128
PAIR = 2 * HD
MIB = 1 << 20
VMEM = pl.BlockSpec(memory_space=pltpu.VMEM)
HBM = pl.BlockSpec(memory_space=pltpu.HBM)
AXES = ("grp", "ctx")


def in_vmem(x):
    return pltpu.with_memory_space_constraint(x, pltpu.VMEM)


def in_hbm(x):
    return pltpu.with_memory_space_constraint(x, pltpu.HBM)


def params(mib):
    return pltpu.CompilerParams(vmem_limit_bytes=mib * MIB)


def cost(us):
    return pl.CostEstimate(flops=int(us * 1e9), bytes_accessed=int(us * 3e6), transcendentals=0)


def dot(a, b, dims):
    return lax.dot_general(a, b, (dims, ((), ())), preferred_element_type=jnp.float32)


def parity(rows, width):
    return lax.rem(lax.broadcasted_iota(jnp.int32, (rows, width), 0), 2)


def by_head(x):
    odd = parity(16, HD).astype(jnp.bfloat16)
    tiles = x.reshape(-1, 16, HD)
    halves = [(tiles * m[None]).reshape(x.shape) for m in (1 - odd, odd)]
    return jnp.concatenate(halves, axis=1)


def paired(x):
    return x.reshape(x.shape[0], -1, HD)


def call(body, us, mib, inputs, outputs, scratch=(), aliases=None):
    return pl.pallas_call(
        body,
        in_specs=[VMEM if v else HBM for _, v in inputs],
        out_specs=[VMEM if v else HBM for _, _, v in outputs],
        out_shape=[(pltpu.VMEM if v else pltpu.HBM)(s, t) for s, t, v in outputs],
        scratch_shapes=list(scratch),
        input_output_aliases=aliases or {},
        compiler_params=params(mib),
        cost_estimate=cost(us),
    )(*[in_vmem(x) if v else in_hbm(x) for x, v in inputs])


def gets(ins, outs, sem, first, pairs):
    return [
        pltpu.make_async_copy(src.at[:, first + m], dst.at[m], sem.at[i, m])
        for i, (src, dst) in enumerate(zip(ins, outs))
        for m in range(pairs)
    ]


def start(copies):
    for c in copies:
        c.start()


def wait(copies):
    for c in copies:
        c.wait()


def fetch_shapes(n, pairs, tokens):
    return [((pairs, tokens, 2, HD), jnp.bfloat16, True)] * n


def relay(arrays, first, pairs):
    n, tokens = len(arrays), arrays[0].shape[0]

    def body(*refs):
        copies = gets(refs[:n], refs[n : 2 * n], refs[-1], first, pairs)
        start(copies)
        wait(copies)

    sems = [pltpu.SemaphoreType.DMA((n, pairs))]
    outs = call(body, 1, 1, [(a, False) for a in arrays], fetch_shapes(n, pairs, tokens), sems)
    return list(map(paired, outs))


def totals(k, v, first, sums, heads, arrays, then):
    pairs, rows, _ = k.shape
    n = len(arrays) if then else 0
    held = sums is not None

    def body(k_ref, v_ref, *refs):
        refs = refs[held:]
        ins, o_ref, outs = refs[:n], refs[n], refs[n + 1 : 2 * n + 1]
        mine, sem, got = refs[2 * n + 1 :]
        copies = gets(ins, outs, got, *then) if then else []
        start(copies)

        def step(m, carry):
            s = dot(k_ref[m], by_head(v_ref[m]), ((0,), (0,)))
            mine[2 * m] = s[:, :HD]
            mine[2 * m + 1] = s[:, HD:]
            return carry

        lax.fori_loop(0, pairs, step, 0)
        out = pltpu.make_async_copy(mine, o_ref.at[pl.ds(2 * first, 2 * pairs)], sem)
        out.start()
        out.wait()
        wait(copies)

    inputs = [(k, True), (v, True)] + ([(sums, False)] if held else [])
    inputs += [(a, False) for a in arrays[:n]]
    outputs = [((heads, HD, HD), jnp.float32, False)]
    if then:
        outputs += fetch_shapes(n, then[1], rows // 2)
    scratch = [
        pltpu.VMEM((2 * pairs, HD, HD), jnp.float32),
        pltpu.SemaphoreType.DMA,
        pltpu.SemaphoreType.DMA((max(n, 1), then[1] if then else 1)),
    ]
    sums, *got = call(body, 2, 4, inputs, outputs, scratch, {2: 0} if held else None)
    return sums, list(map(paired, got))


def local(q, k, v, first, kept, arrays, then):
    pairs, rows, _ = q.shape
    blocks = rows // PAIR
    n = len(arrays) if then else 0
    every = arrays[0].shape[1]
    held = 2 if kept else 0

    def body(q_ref, k_ref, v_ref, *refs):
        refs = refs[held:]
        ins, x_ref, p_ref, outs = refs[:n], refs[n], refs[n + 1], refs[n + 2 : 2 * n + 2]
        mask, score, states, mine, sem, got = refs[2 * n + 2 :]
        copies = gets(ins, outs, got, *then) if then else []
        here = pl.ds(first, pairs)
        copies.append(pltpu.make_async_copy(q_ref, p_ref.at[here], sem.at[0]))
        start(copies)
        i = lax.broadcasted_iota(jnp.int32, (PAIR, PAIR), 0)
        j = lax.broadcasted_iota(jnp.int32, (PAIR, PAIR), 1)
        seen = (i >= j) & (lax.rem(i, 2) == lax.rem(j, 2))
        mask[...] = jnp.where(seen, 1.0, 0.0).astype(jnp.bfloat16)

        def step(m, carry):
            cuts = [pl.ds(c * PAIR, PAIR) for c in range(blocks)]
            for c, at in enumerate(cuts):
                s = dot(q_ref[m, at], k_ref[m, at], ((1,), (1,)))
                score[c] = s.astype(jnp.bfloat16) * mask[...]
            state = None
            for c, at in enumerate(cuts[:-1]):
                piece = dot(k_ref[m, at], by_head(v_ref[m, at]), ((0,), (0,)))
                state = piece if state is None else state + piece
                held = state.astype(jnp.bfloat16)
                states[c, :HD] = held[:, :HD]
                states[c, HD:] = held[:, HD:]
            for c, at in enumerate(cuts):
                x = dot(score[c], v_ref[m, at], ((1,), (0,)))
                if c > 0:
                    x += dot(by_head(q_ref[m, at]), states[c - 1], ((1,), (0,)))
                mine[m, at] = x.astype(jnp.bfloat16)
            return carry

        lax.fori_loop(0, pairs, step, 0)
        out = pltpu.make_async_copy(mine, x_ref.at[here], sem.at[1])
        out.start()
        out.wait()
        wait(copies)

    inputs = [(q, True), (k, True), (v, True)] + [(x, False) for x in kept or ()]
    inputs += [(a, False) for a in arrays[:n]]
    outputs = [((every, rows, HD), jnp.bfloat16, False)] * 2
    if then:
        outputs += fetch_shapes(n, then[1], rows // 2)
    scratch = [
        pltpu.VMEM((PAIR, PAIR), jnp.bfloat16),
        pltpu.VMEM((blocks, PAIR, PAIR), jnp.bfloat16),
        pltpu.VMEM((blocks - 1, PAIR, HD), jnp.bfloat16),
        pltpu.VMEM((pairs, rows, HD), jnp.bfloat16),
        pltpu.SemaphoreType.DMA((2,)),
        pltpu.SemaphoreType.DMA((max(n, 1), then[1] if then else 1)),
    ]
    outs = call(body, 5, 6, inputs, outputs, scratch, {3: 0, 4: 1} if kept else None)
    return outs[:2], list(map(paired, outs[2:]))


def scan(parts):
    devices, pieces = parts.shape[0], 4
    each = devices // pieces

    def body(x_ref, o_ref, mine, sem):
        def step(i, carry):
            mine[i] = carry
            return carry + x_ref[i]

        carry, copies = jnp.zeros(parts.shape[1:], jnp.float32), []
        for p in range(pieces):
            carry = lax.fori_loop(p * each, (p + 1) * each, step, carry, unroll=8)
            here = pl.ds(p * each, each)
            copies.append(pltpu.make_async_copy(mine.at[here], o_ref.at[here], sem.at[p]))
            copies[-1].start()
        wait(copies)

    scratch = [pltpu.VMEM(parts.shape, jnp.float32), pltpu.SemaphoreType.DMA((pieces,))]
    out = [(parts.shape, jnp.float32, False)]
    return call(body, 2, 4, [(parts, True)], out, scratch)[0]


def exchange(x):
    n = lax.axis_size("grp") * lax.axis_size("ctx")
    return lax.all_to_all(x.reshape(n, -1, HD), AXES, 0, 0)


def rows_of(ref, first, rows):
    return ref.at[:, pl.ds(first, rows)]


def first_part(prefix, mixed, q, rows):
    pairs = q.shape[0]

    def body(p_ref, x_ref, q_ref, held_ref, x_out, q_out, sem):
        copies = [
            pltpu.make_async_copy(rows_of(x_ref, 0, rows), x_out, sem.at[0]),
            pltpu.make_async_copy(rows_of(q_ref, 0, rows), q_out, sem.at[1]),
        ]
        start(copies)

        def step(m, carry):
            held_ref[m] = p_ref[m].astype(jnp.bfloat16)
            return carry

        lax.fori_loop(0, 2 * pairs, step, 0)
        wait(copies)

    part = ((pairs, rows, HD), jnp.bfloat16, True)
    return call(
        body,
        3,
        4,
        [(prefix, True), (mixed, False), (q, False)],
        [((2 * pairs, HD, HD), jnp.bfloat16, True), part, part],
        [pltpu.SemaphoreType.DMA((2,))],
    )


def put_out(x_ref, o_ref, sem, first):
    pairs, tokens = x_ref.shape[:2]
    here = pl.ds(first, tokens)
    return [pltpu.make_async_copy(x_ref.at[m], o_ref.at[here, m], sem.at[m]) for m in range(pairs)]


def normed(cuts, part, held, x, q, gain, mixed, every_q, ready, out):
    pairs, rows, _ = q.shape
    tokens = rows // 2
    last, begun = part == len(cuts) - 2, out is not None
    following = 0 if last else cuts[part + 2] - cuts[part + 1]
    late = ready is not None
    entries = 2 * HD * pairs

    def body(held_ref, x_ref, q_ref, g_ref, *refs):
        refs = list(refs)
        more = [] if last else [refs.pop(0), refs.pop(0)]
        done_ref = refs.pop(0) if late else None
        if begun:
            refs.pop(0)
        n_ref = refs.pop(0)
        into = [] if last else [refs.pop(0), refs.pop(0)]
        o_ref = refs.pop(0) if late else None
        kept, sem, put = refs
        copies = [
            pltpu.make_async_copy(rows_of(src, cuts[part + 1], following), dst, sem.at[i])
            for i, (src, dst) in enumerate(zip(more, into))
        ]
        if late:
            copies += put_out(done_ref, o_ref, put, cuts[part - 1] // 2)
        start(copies)
        par = parity(PAIR, HD)

        def step(c, carry):
            at = pl.ds(pl.multiple_of(c * PAIR, PAIR), PAIR)
            total = jnp.zeros((PAIR, HD), jnp.float32)
            for m in range(pairs):
                state = held_ref[2 * m : 2 * m + 2].reshape(PAIR, HD)
                y = x_ref[m, at].astype(jnp.float32) + dot(by_head(q_ref[m, at]), state, ((1,), (0,)))
                kept[m] = y
                total += y * y
            both = total + jnp.where(par == 0, pltpu.roll(total, PAIR - 1, 0), pltpu.roll(total, 1, 0))
            mean = jnp.sum(both, axis=1, keepdims=True) / entries
            scale = jnp.broadcast_to(lax.rsqrt(mean + 1e-06), (PAIR, HD))
            for m in range(pairs):
                y = (kept[m] * scale).reshape(PAIR // 8, 8, HD) * g_ref[m][None]
                n_ref[m, at] = y.reshape(PAIR, HD).astype(jnp.bfloat16)
            return carry

        lax.fori_loop(0, rows // PAIR, step, 0)
        wait(copies)

    inputs = [(held, True), (x, True), (q, True), (gain, True)]
    outputs = [((pairs, rows, HD), jnp.bfloat16, True)]
    if not last:
        piece = ((pairs, following, HD), jnp.bfloat16, True)
        inputs += [(mixed, False), (every_q, False)]
        outputs += [piece, piece]
    aliases = {}
    if late:
        inputs.append((ready, True))
        if begun:
            aliases = {len(inputs): len(outputs)}
            inputs.append((out, False))
        outputs.append(((cuts[-1] // 2, pairs, 2, HD), jnp.bfloat16, False))
    scratch = [
        pltpu.VMEM((pairs, PAIR, HD), jnp.float32),
        pltpu.SemaphoreType.DMA((2,)),
        pltpu.SemaphoreType.DMA((pairs,)),
    ]
    outs = list(call(body, 3, 6, inputs, outputs, scratch, aliases))
    ready = outs.pop(0).reshape(pairs, tokens, 2, HD)
    x, q = (None, None) if last else (outs.pop(0), outs.pop(0))
    return x, q, ready, outs.pop(0) if late else None


def relay_out(ready, out, first):
    def body(x_ref, _, o_ref, sem):
        copies = put_out(x_ref, o_ref, sem, first)
        start(copies)
        wait(copies)

    return call(
        body,
        1,
        1,
        [(ready, True), (out, False)],
        [(out.shape, out.dtype, False)],
        [pltpu.SemaphoreType.DMA((ready.shape[0],))],
        {1: 0},
    )[0]


def attend(queries, keys, values, norm_gain):
    tokens, heads, width = queries.shape
    pairs = heads // 2
    q4, k4, v4 = (x.reshape(tokens, pairs, 2, width) for x in (queries, keys, values))

    cuts = [0, 2, 6, 11, 16]
    k, v = relay([k4, v4], 0, cuts[1])
    sums = None
    for i in range(len(cuts) - 1):
        then = (cuts[i + 1], cuts[i + 2] - cuts[i + 1]) if i + 2 < len(cuts) else None
        sums, got = totals(k, v, cuts[i], sums, heads, [k4, v4], then)
        k, v = got or (None, None)
    parts = exchange(sums)
    sums = scan(parts)
    prefix = exchange(sums).reshape(heads, width, width)

    kept = None
    for half in range(2):
        step = pairs // 4
        now = relay([q4, k4, v4], 2 * half * step, step)
        for i in range(2):
            then = ((2 * half + 1) * step, step) if i == 0 else None
            kept, now = local(*now, (2 * half + i) * step, kept, [q4, k4, v4], then)
    mixed, every_q = kept

    cuts = [0, PAIR, 3 * PAIR, 5 * PAIR, 6 * PAIR]
    gain = jnp.tile(norm_gain.reshape(pairs, 2, width), (1, 4, 1))
    held, x, q = first_part(prefix, mixed, every_q, cuts[1])
    ready, out = None, None
    for part in range(len(cuts) - 1):
        x, q, ready, out = normed(cuts, part, held, x, q, gain, mixed, every_q, ready, out)
    out = relay_out(ready, out, cuts[-2] // 2)
    return out.reshape(tokens, heads, width)


def solution(mesh):
    spec = P(AXES, None, None)
    return jax.shard_map(
        attend, mesh=mesh, in_specs=(spec, spec, spec, P()), out_specs=spec, check_vma=False
    )
```

time: 891 us -> 101 us (0.11)
  waiting for transfers between devices: 783 us -> 3.8 us
  matrix products: 50.6 us -> 0 us
  Pallas kernels: 0 us -> 49.4 us
  blocking collectives: 0 us -> 39.6 us
  other arithmetic: 23.1 us -> 0 us
  local copies, waits for them, and re-layouts: 16.1 us -> 0.02 us
  between operations: 13.5 us -> 0.16 us
    all_gather x1 -> x0, waiting for transfers between devices: 515 us -> none  [carried_in(): gathered = lax.all_gather(part, axis)]
    psum x1 -> x0, waiting for transfers between devices: 267 us -> none  [spread(): return lax.psum(kept, axis)]
    dot_general x3 -> x0, matrix products: 50.6 us -> none  [the longest x1 21 us: per_device(): jnp.einsum('cqhd,chde->cqhe', qs, states, preferred_element_type=jnp.floa...]
    pallas_call x0 -> x18, Pallas kernels: none -> 49.4 us  [call(): pl.pallas_call(body, in_specs=[VMEM if v else HBM for _, v in inputs], ou...]
    all_to_all x0 -> x1, blocking collectives: none -> 39.6 us  [exchange(): return lax.all_to_all(x.reshape(n, -1, HD), AXES, 0, 0)]
    convert_element_type x1 -> x0, other arithmetic: 9.64 us -> none  [per_device(): return normed.astype(jnp.bfloat16).reshape(rows, heads, width)]
    reshape x1 -> x0, local copies, waits for them, and re-layouts: 9.1 us -> none  [per_device(): ks = keys.reshape(count, BLOCK, heads, width)]
  transfers between devices with their start and end apart: 3 -> 1, of which waited for: 2 -> 1; matrix products, arithmetic and copies ran while one was open for 3% -> 0% of each run, Pallas kernels for 0% -> 25%
where the time goes in v1:
time: 101 us; the launch traced here: 99.6 us
  Pallas kernels  49.4 us (49%)
  blocking collectives  39.6 us (39%)
  starting transfers between devices  6.67 us (7%)
  waiting for transfers between devices  3.8 us (4%)
    pallas_call x18, Pallas kernels, call(): pl.pallas_call(body, in_specs=[VMEM if v else HBM for _, v in inputs], ou...  49.4 us
    all_to_all x1, blocking collectives, exchange(): return lax.all_to_all(x.reshape(n, -1, HD), AXES, 0, 0)  39.6 us
    all_to_all x1, starting transfers between devices, exchange(): return lax.all_to_all(x.reshape(n, -1, HD), AXES, 0, 0)  6.67 us
    all_to_all x1, waiting for transfers between devices, exchange(): return lax.all_to_all(x.reshape(n, -1, HD), AXES, 0, 0)  3.8 us
  transfers between devices with their start and end apart: 1, of which 1 were waited for; matrix products, arithmetic and copies ran while one was open for 0% of the time, Pallas kernels for 25%

profile of v1, /device:TPU:0, one launch (start us, length us, event | category | flops | bytes accessed | tf_op | source)
XLA Modules:
  0.0 99.6 jit_solution(3579531158855809143)
XLA Ops:
  0.0 1.4 %shard_map.46 = (bf16[2,768,2,128]{3,2,1,0:T(2,128)(2,1)S(1)}, bf16[2,768,2,128]{3,2,1,0:T(2,128)(2,1)S(1)}) custom-call(bf16[768,16,2,128]{3,2,1,0:T(2,128)(2,1)} %bitcast.61, bf16[768,16,2,128]{3,2,1,0:T(2,128)(2,1)} %bitcast.69), custom_call_target="tpu_custom_call" | custom-call | flops 1000000000 | bytes 3000000 | tf_op jit(solution)/shard_map/pallas_call | solution.py:53
  1.4 2.1 %shard_map.47 = (f32[32,128,128]{2,1,0:T(8,128)}, bf16[4,768,2,128]{3,2,1,0:T(2,128)(2,1)S(1)}, bf16[4,768,2,128]{3,2,1,0:T(2,128)(2,1)S(1)}) custom-call(bf16[2,1536,128]{2,1,0:T(8,128)(2,1)S(1)} %bitcast.53, bf16[2,1536,128]{2,1,0:T(8,128)(2,1)S(1)} %bitcast.54, bf16[768,16,2,128]{3,2,1,0:T(2,128)(2,1)} %bitcast.62, bf16[768,16,2,128]{3,2,1,0:T(2,128)(2,1)} %bitcast.70), custom_call_target="tpu_custom_call" | custom-call | flops 2000000000 | bytes 6000000 | tf_op jit(solution)/shard_map/pallas_call | solution.py:53
  3.6 2.5 %shard_map.48 = (f32[32,128,128]{2,1,0:T(8,128)}, bf16[5,768,2,128]{3,2,1,0:T(2,128)(2,1)S(1)}, bf16[5,768,2,128]{3,2,1,0:T(2,128)(2,1)S(1)}) custom-call(bf16[4,1536,128]{2,1,0:T(8,128)(2,1)S(1)} %bitcast.49, bf16[4,1536,128]{2,1,0:T(8,128)(2,1)S(1)} %bitcast.50, f32[32,128,128]{2,1,0:T(8,128)} %get-tuple-element.56.refs_0_, ...), custom_call_target="tpu_custom_call", output_to_operand_aliasing={{0}: (2, {})} | custom-call | flops 2000000000 | bytes 6000000 | tf_op jit(solution)/shard_map/pallas_call | solution.py:53
  6.0 2.5 %shard_map.49 = (f32[32,128,128]{2,1,0:T(8,128)}, bf16[5,768,2,128]{3,2,1,0:T(2,128)(2,1)S(1)}, bf16[5,768,2,128]{3,2,1,0:T(2,128)(2,1)S(1)}) custom-call(bf16[5,1536,128]{2,1,0:T(8,128)(2,1)S(1)} %bitcast.35, bf16[5,1536,128]{2,1,0:T(8,128)(2,1)S(1)} %bitcast.36, f32[32,128,128]{2,1,0:T(8,128)} %get-tuple-element.59.refs_0_, ...), custom_call_target="tpu_custom_call", output_to_operand_aliasing={{0}: (2, {})} | custom-call | flops 2000000000 | bytes 6000000 | tf_op jit(solution)/shard_map/pallas_call | solution.py:53
  8.6 2.4 %shard_map.50 = f32[32,128,128]{2,1,0:T(8,128)} custom-call(bf16[5,1536,128]{2,1,0:T(8,128)(2,1)S(1)} %bitcast.37, bf16[5,1536,128]{2,1,0:T(8,128)(2,1)S(1)} %bitcast.38, f32[32,128,128]{2,1,0:T(8,128)} %get-tuple-element.62.refs_0_), custom_call_target="tpu_custom_call", output_to_operand_aliasing={{}: (2, {})} | custom-call | flops 2000000000 | bytes 6000000 | tf_op jit(solution)/shard_map/pallas_call | solution.py:53
  11.0 39.6 %all_to_all.10.x_ref = f32[128,32,128]{2,1,0:T(8,128)S(1)} all-to-all(f32[128,32,128]{2,1,0:T(8,128)} %bitcast.81), channel_id=1, replica_groups=mesh['grp'=2,'ctx'=64] {'grp','ctx'}, dimensions={0} | all-to-all | bytes 4194304 | tf_op jit(solution)/shard_map/all_to_all | solution.py:224
  50.6 1.4 %shard_map.51 = f32[128,32,128]{2,1,0:T(8,128)} custom-call(f32[128,32,128]{2,1,0:T(8,128)S(1)} %all_to_all.10.x_ref), custom_call_target="tpu_custom_call" | custom-call | flops 2000000000 | bytes 6000000 | tf_op jit(solution)/shard_map/pallas_call | solution.py:53
  52.0 6.7 %all-to-all-start.1 = ((f32[128,32,128]{2,1,0:T(8,128)}), f32[128,32,128]{2,1,0:T(8,128)S(1)}, u32[]{:S(2)}, u32[]{:S(2)}) async-start(f32[128,32,128]{2,1,0:T(8,128)} %shard_map.51), calls=%async_computation.1 | async-start | bytes 4194304 | tf_op jit(solution)/shard_map/all_to_all | solution.py:224
  58.7 2.6 %shard_map.53 = (bf16[4,768,2,128]{3,2,1,0:T(2,128)(2,1)S(1)}, bf16[4,768,2,128]{3,2,1,0:T(2,128)(2,1)S(1)}, bf16[4,768,2,128]{3,2,1,0:T(2,128)(2,1)S(1)}) custom-call(bf16[768,16,2,128]{3,2,1,0:T(2,128)(2,1)} %bitcast.77, bf16[768,16,2,128]{3,2,1,0:T(2,128)(2,1)} %bitcast.65, bf16[768,16,2,128]{3,2,1,0:T(2,128)(2,1)} %bitcast.73), custom_call_target="tpu_custom_call" | custom-call | flops 1000000000 | bytes 3000000 | tf_op jit(solution)/shard_map/pallas_call | solution.py:53
  61.3 2.6 %shard_map.52 = (bf16[4,768,2,128]{3,2,1,0:T(2,128)(2,1)S(1)}, bf16[4,768,2,128]{3,2,1,0:T(2,128)(2,1)S(1)}, bf16[4,768,2,128]{3,2,1,0:T(2,128)(2,1)S(1)}) custom-call(bf16[768,16,2,128]{3,2,1,0:T(2,128)(2,1)} %bitcast.78, bf16[768,16,2,128]{3,2,1,0:T(2,128)(2,1)} %bitcast.66, bf16[768,16,2,128]{3,2,1,0:T(2,128)(2,1)} %bitcast.74), custom_call_target="tpu_custom_call" | custom-call | flops 1000000000 | bytes 3000000 | tf_op jit(solution)/shard_map/pallas_call | solution.py:53
  63.9 4.9 %shard_map.54 = (bf16[16,1536,128]{2,1,0:T(8,128)(2,1)}, bf16[16,1536,128]{2,1,0:T(8,128)(2,1)}, bf16[4,768,2,128]{3,2,1,0:T(2,128)(2,1)S(1)}, bf16[4,768,2,128]...) custom-call(bf16[4,1536,128]{2,1,0:T(8,128)(2,1)S(1)} %bitcast.46, bf16[4,1536,128]{2,1,0:T(8,128)(2,1)S(1)} %bitcast.47, ...), custom_call_target="tpu_custom_call" | custom-call | flops 5000000000 | bytes 15000000 | tf_op jit(solution)/shard_map/pallas_call | solution.py:53
  68.8 4.8 %shard_map.55 = (bf16[16,1536,128]{2,1,0:T(8,128)(2,1)}, bf16[16,1536,128]{2,1,0:T(8,128)(2,1)}) custom-call(bf16[4,1536,128]{2,1,0:T(8,128)(2,1)S(1)} %bitcast.58, bf16[4,1536,128]{2,1,0:T(8,128)(2,1)S(1)} %bitcast.59, bf16[4,1536,128]{2,1,0:T(8,128)(2,1)S(1)} %bitcast.60, ...), custom_call_target="tpu_custom_call", output_to_operand_aliasing={{0}: (3, {}), {1}: (4, {})} | custom-call | flops 5000000000 | bytes 15000000 | tf_op jit(solution)/shard_map/pallas_call | solution.py:53
  73.6 4.9 %shard_map.56 = (bf16[16,1536,128]{2,1,0:T(8,128)(2,1)}, bf16[16,1536,128]{2,1,0:T(8,128)(2,1)}, bf16[4,768,2,128]{3,2,1,0:T(2,128)(2,1)S(1)}, bf16[4,768,2,128]...) custom-call(bf16[4,1536,128]{2,1,0:T(8,128)(2,1)S(1)} %bitcast.43, ...), custom_call_target="tpu_custom_call", output_to_operand_aliasing={{0}: (3, {}), {1}: (4, {})} | custom-call | flops 5000000000 | bytes 15000000 | tf_op jit(solution)/shard_map/pallas_call | solution.py:53
  78.5 4.8 %shard_map.57 = (bf16[16,1536,128]{2,1,0:T(8,128)(2,1)}, bf16[16,1536,128]{2,1,0:T(8,128)(2,1)}) custom-call(bf16[4,1536,128]{2,1,0:T(8,128)(2,1)S(1)} %bitcast.55, bf16[4,1536,128]{2,1,0:T(8,128)(2,1)S(1)} %bitcast.56, bf16[4,1536,128]{2,1,0:T(8,128)(2,1)S(1)} %bitcast.57, ...), custom_call_target="tpu_custom_call", output_to_operand_aliasing={{0}: (3, {}), {1}: (4, {})} | custom-call | flops 5000000000 | bytes 15000000 | tf_op jit(solution)/shard_map/pallas_call | solution.py:53
  83.3 3.8 %all-to-all-done.1 = f32[128,32,128]{2,1,0:T(8,128)S(1)} async-done(((f32[128,32,128]{2,1,0:T(8,128)}), f32[128,32,128]{2,1,0:T(8,128)S(1)}, u32[]{:S(2)}, u32[]{:S(2)}) %all-to-all-start.1) | async-done | bytes 2097184 | tf_op jit(solution)/shard_map/all_to_all | solution.py:224
  87.1 0.0 copy-start
  87.1 1.6 %shard_map.58 = (bf16[32,128,128]{2,1,0:T(8,128)(2,1)S(1)}, bf16[16,256,128]{2,1,0:T(8,128)(2,1)S(1)}, bf16[16,256,128]{2,1,0:T(8,128)(2,1)S(1)}) custom-call(f32[32,128,128]{2,1,0:T(8,128)S(1)} %bitcast.32, bf16[16,1536,128]{2,1,0:T(8,128)(2,1)} %get-tuple-element.81.x_ref.refs_0_, bf16[16,1536,128]{2,1,0:T(8,128)(2,1)} %get-tuple-element.82.q_ref.refs_1_), custom_call_target="tpu_custom_call" | custom-call | flops 3000000000 | bytes 9000000 | tf_op jit(solution)/shard_map/pallas_call | solution.py:53
  88.7 0.0 copy-done
  88.7 2.4 %shard_map.59 = (bf16[16,256,128]{2,1,0:T(8,128)(2,1)S(1)}, bf16[16,512,128]{2,1,0:T(8,128)(2,1)S(1)}, bf16[16,512,128]{2,1,0:T(8,128)(2,1)S(1)}) custom-call(bf16[32,128,128]{2,1,0:T(8,128)(2,1)S(1)} %get-tuple-element.83.held_ref, bf16[16,256,128]{2,1,0:T(8,128)(2,1)S(1)} %get-tuple-element.84.x_ref, bf16[16,256,128]{2,1,0:T(8,128)(2,1)S(1)} %get-tuple-element.85.q_ref, ...), custom_call_target="tpu_custom_call" | custom-call | flops 3000000000 | bytes 9000000 | tf_op jit(solution)/shard_map/pallas_call | solution.py:53
  91.1 2.8 %shard_map.60 = (bf16[16,512,128]{2,1,0:T(8,128)(2,1)S(1)}, bf16[16,512,128]{2,1,0:T(8,128)(2,1)S(1)}, bf16[16,512,128]{2,1,0:T(8,128)(2,1)S(1)}, bf16[768,16,2,128]{3,2,1,0:T(2,128)(2,1)}) custom-call(bf16[32,128,128]{2,1,0:T(8,128)(2,1)S(1)} %get-tuple-element.83.held_ref, bf16[16,512,128]{2,1,0:T(8,128)(2,1)S(1)} %get-tuple-element.86.x_ref, ...), custom_call_target="tpu_custom_call" | custom-call | flops 3000000000 | bytes 9000000 | tf_op jit(solution)/shard_map/pallas_call | solution.py:53
  93.9 2.5 %shard_map.61 = (bf16[16,512,128]{2,1,0:T(8,128)(2,1)S(1)}, bf16[16,256,128]{2,1,0:T(8,128)(2,1)S(1)}, bf16[16,256,128]{2,1,0:T(8,128)(2,1)S(1)}, bf16[768,16,2,128]{3,2,1,0:T(2,128)(2,1)}) custom-call(bf16[32,128,128]{2,1,0:T(8,128)(2,1)S(1)} %get-tuple-element.83.held_ref, ...), custom_call_target="tpu_custom_call", output_to_operand_aliasing={{3}: (7, {})} | custom-call | flops 3000000000 | bytes 9000000 | tf_op jit(solution)/shard_map/pallas_call | solution.py:53
  96.4 2.1 %shard_map.62 = (bf16[16,256,128]{2,1,0:T(8,128)(2,1)S(1)}, bf16[768,16,2,128]{3,2,1,0:T(2,128)(2,1)}) custom-call(bf16[32,128,128]{2,1,0:T(8,128)(2,1)S(1)} %get-tuple-element.83.held_ref, bf16[16,256,128]{2,1,0:T(8,128)(2,1)S(1)} %get-tuple-element.93.x_ref, bf16[16,256,128]{2,1,0:T(8,128)(2,1)S(1)} %get-tuple-element.94.q_ref, ...), custom_call_target="tpu_custom_call", output_to_operand_aliasing={{1}: (5, {})} | custom-call | flops 3000000000 | bytes 9000000 | tf_op jit(solution)/shard_map/pallas_call | solution.py:53
  98.5 1.1 %shard_map.63 = bf16[768,16,2,128]{3,2,1,0:T(2,128)(2,1)} custom-call(bf16[16,128,2,128]{3,2,1,0:T(2,128)(2,1)S(1)} %bitcast.52, bf16[768,16,2,128]{3,2,1,0:T(2,128)(2,1)} %get-tuple-element.98._), custom_call_target="tpu_custom_call", output_to_operand_aliasing={{}: (1, {})} | custom-call | flops 1000000000 | bytes 3000000 | tf_op jit(solution)/shard_map/pallas_call | solution.py:53
  (1 shorter events, 0.0 us)
Async XLA Ops:
  52.0 35.1 %all-to-all-start.1 = ((f32[128,32,128]{2,1,0:T(8,128)}), f32[128,32,128]{2,1,0:T(8,128)S(1)}, u32[]{:S(2)}, u32[]{:S(2)}) async-start(f32[128,32,128]{2,1,0:T(8,128)} %shard_map.51), calls=%async_computation.1 | async-start | bytes 4194304 | tf_op jit(solution)/shard_map/all_to_all | solution.py:224
  87.1 1.6 %copy-start = (f32[4096]{0:T(1024)S(1)}, f32[4096]{0:T(1024)}, u32[]{:S(2)}) copy-start(f32[4096]{0:T(1024)} %param.7) | copy-start | bytes 49156

commit v2 on v1

--- a/solution.py
+++ b/solution.py
@@ -115,10 +115,9 @@
             mine[2 * m + 1] = s[:, HD:]
             return carry
 
-        lax.fori_loop(0, pairs, step, 0)
-        out = pltpu.make_async_copy(mine, o_ref.at[pl.ds(2 * first, 2 * pairs)], sem)
-        out.start()
-        out.wait()
+        lax.fori_loop(0, pairs, step, 0, unroll=True)
+        copies.append(pltpu.make_async_copy(mine, o_ref.at[pl.ds(2 * first, 2 * pairs)], sem))
+        start(copies[-1:])
         wait(copies)
 
     inputs = [(k, True), (v, True)] + ([(sums, False)] if held else [])
@@ -228,34 +227,6 @@
     return ref.at[:, pl.ds(first, rows)]
 
 
-def first_part(prefix, mixed, q, rows):
-    pairs = q.shape[0]
-
-    def body(p_ref, x_ref, q_ref, held_ref, x_out, q_out, sem):
-        copies = [
-            pltpu.make_async_copy(rows_of(x_ref, 0, rows), x_out, sem.at[0]),
-            pltpu.make_async_copy(rows_of(q_ref, 0, rows), q_out, sem.at[1]),
-        ]
-        start(copies)
-
-        def step(m, carry):
-            held_ref[m] = p_ref[m].astype(jnp.bfloat16)
-            return carry
-
-        lax.fori_loop(0, 2 * pairs, step, 0)
-        wait(copies)
-
-    part = ((pairs, rows, HD), jnp.bfloat16, True)
-    return call(
-        body,
-        3,
-        4,
-        [(prefix, True), (mixed, False), (q, False)],
-        [((2 * pairs, HD, HD), jnp.bfloat16, True), part, part],
-        [pltpu.SemaphoreType.DMA((2,))],
-    )
-
-
 def put_out(x_ref, o_ref, sem, first):
     pairs, tokens = x_ref.shape[:2]
     here = pl.ds(first, tokens)
@@ -263,15 +234,16 @@
 
 
 def normed(cuts, part, held, x, q, gain, mixed, every_q, ready, out):
-    pairs, rows, _ = q.shape
-    tokens = rows // 2
+    pairs, rows = every_q.shape[0], cuts[part + 1] - cuts[part]
+    opening = part == 0
     last, begun = part == len(cuts) - 2, out is not None
     following = 0 if last else cuts[part + 2] - cuts[part + 1]
     late = ready is not None
     entries = 2 * HD * pairs
 
-    def body(held_ref, x_ref, q_ref, g_ref, *refs):
+    def body(held_ref, g_ref, *refs):
         refs = list(refs)
+        x_ref, q_ref = (None, None) if opening else (refs.pop(0), refs.pop(0))
         more = [] if last else [refs.pop(0), refs.pop(0)]
         done_ref = refs.pop(0) if late else None
         if begun:
@@ -279,7 +251,16 @@
         n_ref = refs.pop(0)
         into = [] if last else [refs.pop(0), refs.pop(0)]
         o_ref = refs.pop(0) if late else None
-        kept, sem, put = refs
+        wide = held_ref
+        if opening:
+            held_ref, kept, sem, put, x_ref, q_ref, own = refs
+            mine = [
+                pltpu.make_async_copy(rows_of(src, 0, rows), dst, own.at[i])
+                for i, (src, dst) in enumerate(zip(more, (x_ref, q_ref)))
+            ]
+            start(mine)
+        else:
+            kept, sem, put = refs
         copies = [
             pltpu.make_async_copy(rows_of(src, cuts[part + 1], following), dst, sem.at[i])
             for i, (src, dst) in enumerate(zip(more, into))
@@ -287,6 +268,14 @@
         if late:
             copies += put_out(done_ref, o_ref, put, cuts[part - 1] // 2)
         start(copies)
+        if opening:
+
+            def narrow(m, carry):
+                held_ref[m] = wide[m].astype(jnp.bfloat16)
+                return carry
+
+            lax.fori_loop(0, 2 * pairs, narrow, 0, unroll=4)
+            wait(mine)
         par = parity(PAIR, HD)
 
         def step(c, carry):
@@ -308,7 +297,7 @@
         lax.fori_loop(0, rows // PAIR, step, 0)
         wait(copies)
 
-    inputs = [(held, True), (x, True), (q, True), (gain, True)]
+    inputs = [(held, True), (gain, True)] + ([] if opening else [(x, True), (q, True)])
     outputs = [((pairs, rows, HD), jnp.bfloat16, True)]
     if not last:
         piece = ((pairs, following, HD), jnp.bfloat16, True)
@@ -326,10 +315,14 @@
         pltpu.SemaphoreType.DMA((2,)),
         pltpu.SemaphoreType.DMA((pairs,)),
     ]
-    outs = list(call(body, 3, 6, inputs, outputs, scratch, aliases))
-    ready = outs.pop(0).reshape(pairs, tokens, 2, HD)
+    if opening:
+        outputs.append(((2 * pairs, HD, HD), jnp.bfloat16, True))
+        scratch += [pltpu.VMEM((pairs, rows, HD), jnp.bfloat16)] * 2 + [pltpu.SemaphoreType.DMA((2,))]
+    outs = list(call(body, 3, 8, inputs, outputs, scratch, aliases))
+    ready = outs.pop(0).reshape(pairs, rows // 2, 2, HD)
     x, q = (None, None) if last else (outs.pop(0), outs.pop(0))
-    return x, q, ready, outs.pop(0) if late else None
+    out = outs.pop(0) if late else None
+    return outs.pop(0) if opening else held, x, q, ready, out
 
 
 def relay_out(ready, out, first):
@@ -354,7 +347,7 @@
     pairs = heads // 2
     q4, k4, v4 = (x.reshape(tokens, pairs, 2, width) for x in (queries, keys, values))
 
-    cuts = [0, 2, 6, 11, 16]
+    cuts = [0, 7, 14, 16]
     k, v = relay([k4, v4], 0, cuts[1])
     sums = None
     for i in range(len(cuts) - 1):
@@ -376,10 +369,9 @@
 
     cuts = [0, PAIR, 3 * PAIR, 5 * PAIR, 6 * PAIR]
     gain = jnp.tile(norm_gain.reshape(pairs, 2, width), (1, 4, 1))
-    held, x, q = first_part(prefix, mixed, every_q, cuts[1])
-    ready, out = None, None
+    held, x, q, ready, out = prefix, None, None, None, None
     for part in range(len(cuts) - 1):
-        x, q, ready, out = normed(cuts, part, held, x, q, gain, mixed, every_q, ready, out)
+        held, x, q, ready, out = normed(cuts, part, held, x, q, gain, mixed, every_q, ready, out)
     out = relay_out(ready, out, cuts[-2] // 2)
     return out.reshape(tokens, heads, width)
 

time: 101 us -> 98.7 us (0.977)
  Pallas kernels: 49.4 us -> 47.6 us
    pallas_call x18 -> x16, Pallas kernels: 49.4 us -> 47.6 us  [call(): pl.pallas_call(body, in_specs=[VMEM if v else HBM for _, v in inputs], ou...]
where the time goes in v2:
time: 98.7 us; the launch traced here: 97.9 us
  Pallas kernels  47.6 us (48%)
  blocking collectives  39.6 us (40%)
  starting transfers between devices  6.67 us (7%)
  waiting for transfers between devices  3.84 us (4%)
    pallas_call x16, Pallas kernels, call(): pl.pallas_call(body, in_specs=[VMEM if v else HBM for _, v in inputs], ou...  47.6 us
    all_to_all x1, blocking collectives, exchange(): return lax.all_to_all(x.reshape(n, -1, HD), AXES, 0, 0)  39.6 us
    all_to_all x1, starting transfers between devices, exchange(): return lax.all_to_all(x.reshape(n, -1, HD), AXES, 0, 0)  6.67 us
    all_to_all x1, waiting for transfers between devices, exchange(): return lax.all_to_all(x.reshape(n, -1, HD), AXES, 0, 0)  3.84 us
  transfers between devices with their start and end apart: 1, of which 1 were waited for; matrix products, arithmetic and copies ran while one was open for 0% of the time, Pallas kernels for 25%

profile of v2, /device:TPU:0, one launch (start us, length us, event | category | flops | bytes accessed | tf_op | source)
XLA Modules:
  0.0 97.9 jit_solution(10263964186608076029)
XLA Ops:
  0.0 2.9 %shard_map.46 = (bf16[7,768,2,128]{3,2,1,0:T(2,128)(2,1)S(1)}, bf16[7,768,2,128]{3,2,1,0:T(2,128)(2,1)S(1)}) custom-call(bf16[768,16,2,128]{3,2,1,0:T(2,128)(2,1)} %bitcast.57, bf16[768,16,2,128]{3,2,1,0:T(2,128)(2,1)} %bitcast.64), custom_call_target="tpu_custom_call" | custom-call | flops 1000000000 | bytes 3000000 | tf_op jit(solution)/shard_map/pallas_call | solution.py:53
  2.9 4.0 %shard_map.47 = (f32[32,128,128]{2,1,0:T(8,128)}, bf16[7,768,2,128]{3,2,1,0:T(2,128)(2,1)S(1)}, bf16[7,768,2,128]{3,2,1,0:T(2,128)(2,1)S(1)}) custom-call(bf16[7,1536,128]{2,1,0:T(8,128)(2,1)S(1)} %bitcast.33, bf16[7,1536,128]{2,1,0:T(8,128)(2,1)S(1)} %bitcast.34, bf16[768,16,2,128]{3,2,1,0:T(2,128)(2,1)} %bitcast.58, bf16[768,16,2,128]{3,2,1,0:T(2,128)(2,1)} %bitcast.65), custom_call_target="tpu_custom_call" | custom-call | flops 2000000000 | bytes 6000000 | tf_op jit(solution)/shard_map/pallas_call | solution.py:53
  6.9 1.9 %shard_map.48 = (f32[32,128,128]{2,1,0:T(8,128)}, bf16[2,768,2,128]{3,2,1,0:T(2,128)(2,1)S(1)}, bf16[2,768,2,128]{3,2,1,0:T(2,128)(2,1)S(1)}) custom-call(bf16[7,1536,128]{2,1,0:T(8,128)(2,1)S(1)} %bitcast.31, bf16[7,1536,128]{2,1,0:T(8,128)(2,1)S(1)} %bitcast.32, f32[32,128,128]{2,1,0:T(8,128)} %get-tuple-element.51.refs_0_, ...), custom_call_target="tpu_custom_call", output_to_operand_aliasing={{0}: (2, {})} | custom-call | flops 2000000000 | bytes 6000000 | tf_op jit(solution)/shard_map/pallas_call | solution.py:53
  8.8 1.1 %shard_map.49 = f32[32,128,128]{2,1,0:T(8,128)} custom-call(bf16[2,1536,128]{2,1,0:T(8,128)(2,1)S(1)} %bitcast.55, bf16[2,1536,128]{2,1,0:T(8,128)(2,1)S(1)} %bitcast.56, f32[32,128,128]{2,1,0:T(8,128)} %get-tuple-element.54.refs_0_), custom_call_target="tpu_custom_call", output_to_operand_aliasing={{}: (2, {})} | custom-call | flops 2000000000 | bytes 6000000 | tf_op jit(solution)/shard_map/pallas_call | solution.py:53
  9.9 39.6 %all_to_all.10.x_ref = f32[128,32,128]{2,1,0:T(8,128)S(1)} all-to-all(f32[128,32,128]{2,1,0:T(8,128)} %bitcast.75), channel_id=1, replica_groups=mesh['grp'=2,'ctx'=64] {'grp','ctx'}, dimensions={0} | all-to-all | bytes 4194304 | tf_op jit(solution)/shard_map/all_to_all | solution.py:223
  49.5 1.4 %shard_map.50 = f32[128,32,128]{2,1,0:T(8,128)} custom-call(f32[128,32,128]{2,1,0:T(8,128)S(1)} %all_to_all.10.x_ref), custom_call_target="tpu_custom_call" | custom-call | flops 2000000000 | bytes 6000000 | tf_op jit(solution)/shard_map/pallas_call | solution.py:53
  50.9 6.7 %all-to-all-start.1 = ((f32[128,32,128]{2,1,0:T(8,128)}), f32[128,32,128]{2,1,0:T(8,128)S(1)}, u32[]{:S(2)}, u32[]{:S(2)}) async-start(f32[128,32,128]{2,1,0:T(8,128)} %shard_map.50), calls=%async_computation.1 | async-start | bytes 4194304 | tf_op jit(solution)/shard_map/all_to_all | solution.py:223
  57.6 2.6 %shard_map.52 = (bf16[4,768,2,128]{3,2,1,0:T(2,128)(2,1)S(1)}, bf16[4,768,2,128]{3,2,1,0:T(2,128)(2,1)S(1)}, bf16[4,768,2,128]{3,2,1,0:T(2,128)(2,1)S(1)}) custom-call(bf16[768,16,2,128]{3,2,1,0:T(2,128)(2,1)} %bitcast.71, bf16[768,16,2,128]{3,2,1,0:T(2,128)(2,1)} %bitcast.60, bf16[768,16,2,128]{3,2,1,0:T(2,128)(2,1)} %bitcast.67), custom_call_target="tpu_custom_call" | custom-call | flops 1000000000 | bytes 3000000 | tf_op jit(solution)/shard_map/pallas_call | solution.py:53
  60.2 2.6 %shard_map.51 = (bf16[4,768,2,128]{3,2,1,0:T(2,128)(2,1)S(1)}, bf16[4,768,2,128]{3,2,1,0:T(2,128)(2,1)S(1)}, bf16[4,768,2,128]{3,2,1,0:T(2,128)(2,1)S(1)}) custom-call(bf16[768,16,2,128]{3,2,1,0:T(2,128)(2,1)} %bitcast.72, bf16[768,16,2,128]{3,2,1,0:T(2,128)(2,1)} %bitcast.61, bf16[768,16,2,128]{3,2,1,0:T(2,128)(2,1)} %bitcast.68), custom_call_target="tpu_custom_call" | custom-call | flops 1000000000 | bytes 3000000 | tf_op jit(solution)/shard_map/pallas_call | solution.py:53
  62.8 4.9 %shard_map.53 = (bf16[16,1536,128]{2,1,0:T(8,128)(2,1)}, bf16[16,1536,128]{2,1,0:T(8,128)(2,1)}, bf16[4,768,2,128]{3,2,1,0:T(2,128)(2,1)S(1)}, bf16[4,768,2,128]...) custom-call(bf16[4,1536,128]{2,1,0:T(8,128)(2,1)S(1)} %bitcast.44, bf16[4,1536,128]{2,1,0:T(8,128)(2,1)S(1)} %bitcast.45, ...), custom_call_target="tpu_custom_call" | custom-call | flops 5000000000 | bytes 15000000 | tf_op jit(solution)/shard_map/pallas_call | solution.py:53
  67.7 4.7 %shard_map.54 = (bf16[16,1536,128]{2,1,0:T(8,128)(2,1)}, bf16[16,1536,128]{2,1,0:T(8,128)(2,1)}) custom-call(bf16[4,1536,128]{2,1,0:T(8,128)(2,1)S(1)} %bitcast.52, bf16[4,1536,128]{2,1,0:T(8,128)(2,1)S(1)} %bitcast.53, bf16[4,1536,128]{2,1,0:T(8,128)(2,1)S(1)} %bitcast.54, ...), custom_call_target="tpu_custom_call", output_to_operand_aliasing={{0}: (3, {}), {1}: (4, {})} | custom-call | flops 5000000000 | bytes 15000000 | tf_op jit(solution)/shard_map/pallas_call | solution.py:53
  72.4 4.9 %shard_map.55 = (bf16[16,1536,128]{2,1,0:T(8,128)(2,1)}, bf16[16,1536,128]{2,1,0:T(8,128)(2,1)}, bf16[4,768,2,128]{3,2,1,0:T(2,128)(2,1)S(1)}, bf16[4,768,2,128]...) custom-call(bf16[4,1536,128]{2,1,0:T(8,128)(2,1)S(1)} %bitcast.41, ...), custom_call_target="tpu_custom_call", output_to_operand_aliasing={{0}: (3, {}), {1}: (4, {})} | custom-call | flops 5000000000 | bytes 15000000 | tf_op jit(solution)/shard_map/pallas_call | solution.py:53
  77.3 0.0 copy-start
  77.3 4.8 %shard_map.56 = (bf16[16,1536,128]{2,1,0:T(8,128)(2,1)}, bf16[16,1536,128]{2,1,0:T(8,128)(2,1)}) custom-call(bf16[4,1536,128]{2,1,0:T(8,128)(2,1)S(1)} %bitcast.49, bf16[4,1536,128]{2,1,0:T(8,128)(2,1)S(1)} %bitcast.50, bf16[4,1536,128]{2,1,0:T(8,128)(2,1)S(1)} %bitcast.51, ...), custom_call_target="tpu_custom_call", output_to_operand_aliasing={{0}: (3, {}), {1}: (4, {})} | custom-call | flops 5000000000 | bytes 15000000 | tf_op jit(solution)/shard_map/pallas_call | solution.py:53
  82.1 3.8 %all-to-all-done.1 = f32[128,32,128]{2,1,0:T(8,128)S(1)} async-done(((f32[128,32,128]{2,1,0:T(8,128)}), f32[128,32,128]{2,1,0:T(8,128)S(1)}, u32[]{:S(2)}, u32[]{:S(2)}) %all-to-all-start.1) | async-done | bytes 2097184 | tf_op jit(solution)/shard_map/all_to_all | solution.py:223
  86.0 0.0 copy-done
  86.0 3.4 %shard_map.57 = (bf16[16,256,128]{2,1,0:T(8,128)(2,1)S(1)}, bf16[16,512,128]{2,1,0:T(8,128)(2,1)S(1)}, bf16[16,512,128]{2,1,0:T(8,128)(2,1)S(1)}, bf16[32,128,128]{2,1,0:T(8,128)(2,1)S(1)}) custom-call(f32[32,128,128]{2,1,0:T(8,128)S(1)} %bitcast.30, f32[16,8,128]{2,1,0:T(8,128)S(1)} %bitcast.37, bf16[16,1536,128]{2,1,0:T(8,128)(2,1)} %get-tuple-element.73.refs_0_.refs_2_, ...), custom_call_target="tpu_custom_call" | custom-call | flops 3000000000 | bytes 9000000 | tf_op jit(solution)/shard_map/pallas_call | solution.py:53
  89.4 2.8 %shard_map.58 = (bf16[16,512,128]{2,1,0:T(8,128)(2,1)S(1)}, bf16[16,512,128]{2,1,0:T(8,128)(2,1)S(1)}, bf16[16,512,128]{2,1,0:T(8,128)(2,1)S(1)}, bf16[768,16,2,128]{3,2,1,0:T(2,128)(2,1)}) custom-call(bf16[32,128,128]{2,1,0:T(8,128)(2,1)S(1)} %get-tuple-element.75.held_ref, f32[16,8,128]{2,1,0:T(8,128)S(1)} %bitcast.38, ...), custom_call_target="tpu_custom_call" | custom-call | flops 3000000000 | bytes 9000000 | tf_op jit(solution)/shard_map/pallas_call | solution.py:53
  92.2 2.5 %shard_map.59 = (bf16[16,512,128]{2,1,0:T(8,128)(2,1)S(1)}, bf16[16,256,128]{2,1,0:T(8,128)(2,1)S(1)}, bf16[16,256,128]{2,1,0:T(8,128)(2,1)S(1)}, bf16[768,16,2,128]{3,2,1,0:T(2,128)(2,1)}) custom-call(bf16[32,128,128]{2,1,0:T(8,128)(2,1)S(1)} %get-tuple-element.75.held_ref, f32[16,8,128]{2,1,0:T(8,128)S(1)} %bitcast.39, ...), custom_call_target="tpu_custom_call", output_to_operand_aliasing={{3}: (7, {})} | custom-call | flops 3000000000 | bytes 9000000 | tf_op jit(solution)/shard_map/pallas_call | solution.py:53
  94.7 2.1 %shard_map.60 = (bf16[16,256,128]{2,1,0:T(8,128)(2,1)S(1)}, bf16[768,16,2,128]{3,2,1,0:T(2,128)(2,1)}) custom-call(bf16[32,128,128]{2,1,0:T(8,128)(2,1)S(1)} %get-tuple-element.75.held_ref, f32[16,8,128]{2,1,0:T(8,128)S(1)} %bitcast.40, bf16[16,256,128]{2,1,0:T(8,128)(2,1)S(1)} %get-tuple-element.83.refs_0_, ...), custom_call_target="tpu_custom_call", output_to_operand_aliasing={{1}: (5, {})} | custom-call | flops 3000000000 | bytes 9000000 | tf_op jit(solution)/shard_map/pallas_call | solution.py:53
  96.8 1.1 %shard_map.61 = bf16[768,16,2,128]{3,2,1,0:T(2,128)(2,1)} custom-call(bf16[16,128,2,128]{3,2,1,0:T(2,128)(2,1)S(1)} %bitcast.48, bf16[768,16,2,128]{3,2,1,0:T(2,128)(2,1)} %get-tuple-element.88._), custom_call_target="tpu_custom_call", output_to_operand_aliasing={{}: (1, {})} | custom-call | flops 1000000000 | bytes 3000000 | tf_op jit(solution)/shard_map/pallas_call | solution.py:53
  (1 shorter events, 0.0 us)
Async XLA Ops:
  50.9 35.1 %all-to-all-start.1 = ((f32[128,32,128]{2,1,0:T(8,128)}), f32[128,32,128]{2,1,0:T(8,128)S(1)}, u32[]{:S(2)}, u32[]{:S(2)}) async-start(f32[128,32,128]{2,1,0:T(8,128)} %shard_map.50), calls=%async_computation.1 | async-start | bytes 4194304 | tf_op jit(solution)/shard_map/all_to_all | solution.py:223
  77.3 8.7 %copy-start = (f32[4096]{0:T(1024)S(1)}, f32[4096]{0:T(1024)}, u32[]{:S(2)}) copy-start(f32[4096]{0:T(1024)} %param.7) | copy-start | bytes 49156

commit v3 on v2

--- a/solution.py
+++ b/solution.py
@@ -97,16 +97,27 @@
     return list(map(paired, outs))
 
 
-def totals(k, v, first, sums, heads, arrays, then):
+def totals(k, v, first, sums, ready, heads, arrays, then):
     pairs, rows, _ = k.shape
     n = len(arrays) if then else 0
-    held = sums is not None
+    late, held = ready is not None, sums is not None
 
     def body(k_ref, v_ref, *refs):
-        refs = refs[held:]
-        ins, o_ref, outs = refs[:n], refs[n], refs[n + 1 : 2 * n + 1]
-        mine, sem, got = refs[2 * n + 1 :]
+        refs = list(refs)
+        ins = [refs.pop(0) for _ in range(n)]
+        ready_ref = refs.pop(0) if late else None
+        if held:
+            refs.pop(0)
+        mine = refs.pop(0) if then else None
+        o_ref = refs.pop(0) if late else None
+        outs = [refs.pop(0) for _ in range(n)]
+        sem, got = refs[:2]
+        mine = mine if then else refs[2]
         copies = gets(ins, outs, got, *then) if then else []
+        if late:
+            before = ready_ref.shape[0]
+            here = o_ref.at[pl.ds(2 * first - before, before)]
+            copies.append(pltpu.make_async_copy(ready_ref, here, sem.at[0]))
         start(copies)
 
         def step(m, carry):
@@ -116,22 +127,33 @@
             return carry
 
         lax.fori_loop(0, pairs, step, 0, unroll=True)
-        copies.append(pltpu.make_async_copy(mine, o_ref.at[pl.ds(2 * first, 2 * pairs)], sem))
-        start(copies[-1:])
-        wait(copies)
-
-    inputs = [(k, True), (v, True)] + ([(sums, False)] if held else [])
-    inputs += [(a, False) for a in arrays[:n]]
-    outputs = [((heads, HD, HD), jnp.float32, False)]
-    if then:
-        outputs += fetch_shapes(n, then[1], rows // 2)
+        if not then:
+            here = o_ref.at[pl.ds(2 * first, 2 * pairs)]
+            copies.append(pltpu.make_async_copy(mine, here, sem.at[1]))
+            start(copies[-1:])
+        wait(copies)
+
+    inputs = [(k, True), (v, True)] + [(a, False) for a in arrays[:n]]
+    piece, outputs, aliases = ((2 * pairs, HD, HD), jnp.float32), [], {}
     scratch = [
-        pltpu.VMEM((2 * pairs, HD, HD), jnp.float32),
-        pltpu.SemaphoreType.DMA,
+        pltpu.SemaphoreType.DMA((2,)),
         pltpu.SemaphoreType.DMA((max(n, 1), then[1] if then else 1)),
     ]
-    sums, *got = call(body, 2, 4, inputs, outputs, scratch, {2: 0} if held else None)
-    return sums, list(map(paired, got))
+    if then:
+        outputs.append((*piece, True))
+    else:
+        scratch.append(pltpu.VMEM(*piece))
+    if late:
+        inputs.append((ready, True))
+        if held:
+            aliases = {len(inputs): len(outputs)}
+            inputs.append((sums, False))
+        outputs.append(((heads, HD, HD), jnp.float32, False))
+    outputs += fetch_shapes(n, then[1] if then else 0, rows // 2)
+    outs = list(call(body, 2, 4, inputs, outputs, scratch, aliases))
+    ready = outs.pop(0) if then else None
+    sums = outs.pop(0) if late else None
+    return sums, ready, list(map(paired, outs))
 
 
 def local(q, k, v, first, kept, arrays, then):
@@ -349,10 +371,10 @@
 
     cuts = [0, 7, 14, 16]
     k, v = relay([k4, v4], 0, cuts[1])
-    sums = None
+    sums, ready = None, None
     for i in range(len(cuts) - 1):
         then = (cuts[i + 1], cuts[i + 2] - cuts[i + 1]) if i + 2 < len(cuts) else None
-        sums, got = totals(k, v, cuts[i], sums, heads, [k4, v4], then)
+        sums, ready, got = totals(k, v, cuts[i], sums, ready, heads, [k4, v4], then)
         k, v = got or (None, None)
     parts = exchange(sums)
     sums = scan(parts)

time: 98.7 us -> 98.3 us (level)
  no operation moved by 1% of the time
where the time goes in v3:
time: 98.3 us; the launch traced here: 97.5 us
  Pallas kernels  47.2 us (48%)
  blocking collectives  39.6 us (40%)
  starting transfers between devices  6.67 us (7%)
  waiting for transfers between devices  3.83 us (4%)
    pallas_call x16, Pallas kernels, call(): pl.pallas_call(body, in_specs=[VMEM if v else HBM for _, v in inputs], ou...  47.2 us
    all_to_all x1, blocking collectives, exchange(): return lax.all_to_all(x.reshape(n, -1, HD), AXES, 0, 0)  39.6 us
    all_to_all x1, starting transfers between devices, exchange(): return lax.all_to_all(x.reshape(n, -1, HD), AXES, 0, 0)  6.67 us
    all_to_all x1, waiting for transfers between devices, exchange(): return lax.all_to_all(x.reshape(n, -1, HD), AXES, 0, 0)  3.83 us
  transfers between devices with their start and end apart: 1, of which 1 were waited for; matrix products, arithmetic and copies ran while one was open for 0% of the time, Pallas kernels for 25%

profile of v3, /device:TPU:0, one launch (start us, length us, event | category | flops | bytes accessed | tf_op | source)
XLA Modules:
  0.0 97.5 jit_solution(10728501698666700370)
XLA Ops:
  0.0 2.9 %shard_map.46 = (bf16[7,768,2,128]{3,2,1,0:T(2,128)(2,1)S(1)}, bf16[7,768,2,128]{3,2,1,0:T(2,128)(2,1)S(1)}) custom-call(bf16[768,16,2,128]{3,2,1,0:T(2,128)(2,1)} %bitcast.57, bf16[768,16,2,128]{3,2,1,0:T(2,128)(2,1)} %bitcast.64), custom_call_target="tpu_custom_call" | custom-call | flops 1000000000 | bytes 3000000 | tf_op jit(solution)/shard_map/pallas_call | solution.py:53
  2.9 3.6 %shard_map.47 = (f32[14,128,128]{2,1,0:T(8,128)S(1)}, bf16[7,768,2,128]{3,2,1,0:T(2,128)(2,1)S(1)}, bf16[7,768,2,128]{3,2,1,0:T(2,128)(2,1)S(1)}) custom-call(bf16[7,1536,128]{2,1,0:T(8,128)(2,1)S(1)} %bitcast.33, bf16[7,1536,128]{2,1,0:T(8,128)(2,1)S(1)} %bitcast.34, bf16[768,16,2,128]{3,2,1,0:T(2,128)(2,1)} %bitcast.58, bf16[768,16,2,128]{3,2,1,0:T(2,128)(2,1)} %bitcast.65), custom_call_target="tpu_custom_call" | custom-call | flops 2000000000 | bytes 6000000 | tf_op jit(solution)/shard_map/pallas_call | solution.py:53
  6.5 1.8 %shard_map.48 = (f32[14,128,128]{2,1,0:T(8,128)S(1)}, f32[32,128,128]{2,1,0:T(8,128)}, bf16[2,768,2,128]{3,2,1,0:T(2,128)(2,1)S(1)}, bf16[2,768,2,128]{3,2,1,0:T(2,128)(2,1)S(1)}) custom-call(bf16[7,1536,128]{2,1,0:T(8,128)(2,1)S(1)} %bitcast.31, bf16[7,1536,128]{2,1,0:T(8,128)(2,1)S(1)} %bitcast.32, bf16[768,16,2,128]{3,2,1,0:T(2,128)(2,1)} %bitcast.59, ...), custom_call_target="tpu_custom_call" | custom-call | flops 2000000000 | bytes 6000000 | tf_op jit(solution)/shard_map/pallas_call | solution.py:53
  8.3 1.1 %shard_map.49 = f32[32,128,128]{2,1,0:T(8,128)} custom-call(bf16[2,1536,128]{2,1,0:T(8,128)(2,1)S(1)} %bitcast.55, bf16[2,1536,128]{2,1,0:T(8,128)(2,1)S(1)} %bitcast.56, f32[14,128,128]{2,1,0:T(8,128)S(1)} %get-tuple-element.55.refs_0_, f32[32,128,128]{2,1,0:T(8,128)} %get-tuple-element.56.refs_1_), custom_call_target="tpu_custom_call", output_to_operand_aliasing={{}: (3, {})} | custom-call | flops 2000000000 | bytes 6000000 | tf_op jit(solution)/shard_map/pallas_call | solution.py:53
  9.5 39.6 %all_to_all.10.x_ref = f32[128,32,128]{2,1,0:T(8,128)S(1)} all-to-all(f32[128,32,128]{2,1,0:T(8,128)} %bitcast.75), channel_id=1, replica_groups=mesh['grp'=2,'ctx'=64] {'grp','ctx'}, dimensions={0} | all-to-all | bytes 4194304 | tf_op jit(solution)/shard_map/all_to_all | solution.py:245
  49.1 1.4 %shard_map.50 = f32[128,32,128]{2,1,0:T(8,128)} custom-call(f32[128,32,128]{2,1,0:T(8,128)S(1)} %all_to_all.10.x_ref), custom_call_target="tpu_custom_call" | custom-call | flops 2000000000 | bytes 6000000 | tf_op jit(solution)/shard_map/pallas_call | solution.py:53
  50.5 6.7 %all-to-all-start.1 = ((f32[128,32,128]{2,1,0:T(8,128)}), f32[128,32,128]{2,1,0:T(8,128)S(1)}, u32[]{:S(2)}, u32[]{:S(2)}) async-start(f32[128,32,128]{2,1,0:T(8,128)} %shard_map.50), calls=%async_computation.1 | async-start | bytes 4194304 | tf_op jit(solution)/shard_map/all_to_all | solution.py:245
  57.2 2.6 %shard_map.52 = (bf16[4,768,2,128]{3,2,1,0:T(2,128)(2,1)S(1)}, bf16[4,768,2,128]{3,2,1,0:T(2,128)(2,1)S(1)}, bf16[4,768,2,128]{3,2,1,0:T(2,128)(2,1)S(1)}) custom-call(bf16[768,16,2,128]{3,2,1,0:T(2,128)(2,1)} %bitcast.71, bf16[768,16,2,128]{3,2,1,0:T(2,128)(2,1)} %bitcast.60, bf16[768,16,2,128]{3,2,1,0:T(2,128)(2,1)} %bitcast.67), custom_call_target="tpu_custom_call" | custom-call | flops 1000000000 | bytes 3000000 | tf_op jit(solution)/shard_map/pallas_call | solution.py:53
  59.8 2.6 %shard_map.51 = (bf16[4,768,2,128]{3,2,1,0:T(2,128)(2,1)S(1)}, bf16[4,768,2,128]{3,2,1,0:T(2,128)(2,1)S(1)}, bf16[4,768,2,128]{3,2,1,0:T(2,128)(2,1)S(1)}) custom-call(bf16[768,16,2,128]{3,2,1,0:T(2,128)(2,1)} %bitcast.72, bf16[768,16,2,128]{3,2,1,0:T(2,128)(2,1)} %bitcast.61, bf16[768,16,2,128]{3,2,1,0:T(2,128)(2,1)} %bitcast.68), custom_call_target="tpu_custom_call" | custom-call | flops 1000000000 | bytes 3000000 | tf_op jit(solution)/shard_map/pallas_call | solution.py:53
  62.4 4.9 %shard_map.53 = (bf16[16,1536,128]{2,1,0:T(8,128)(2,1)}, bf16[16,1536,128]{2,1,0:T(8,128)(2,1)}, bf16[4,768,2,128]{3,2,1,0:T(2,128)(2,1)S(1)}, bf16[4,768,2,128]...) custom-call(bf16[4,1536,128]{2,1,0:T(8,128)(2,1)S(1)} %bitcast.44, bf16[4,1536,128]{2,1,0:T(8,128)(2,1)S(1)} %bitcast.45, ...), custom_call_target="tpu_custom_call" | custom-call | flops 5000000000 | bytes 15000000 | tf_op jit(solution)/shard_map/pallas_call | solution.py:53
  67.3 4.7 %shard_map.54 = (bf16[16,1536,128]{2,1,0:T(8,128)(2,1)}, bf16[16,1536,128]{2,1,0:T(8,128)(2,1)}) custom-call(bf16[4,1536,128]{2,1,0:T(8,128)(2,1)S(1)} %bitcast.52, bf16[4,1536,128]{2,1,0:T(8,128)(2,1)S(1)} %bitcast.53, bf16[4,1536,128]{2,1,0:T(8,128)(2,1)S(1)} %bitcast.54, ...), custom_call_target="tpu_custom_call", output_to_operand_aliasing={{0}: (3, {}), {1}: (4, {})} | custom-call | flops 5000000000 | bytes 15000000 | tf_op jit(solution)/shard_map/pallas_call | solution.py:53
  72.0 4.9 %shard_map.55 = (bf16[16,1536,128]{2,1,0:T(8,128)(2,1)}, bf16[16,1536,128]{2,1,0:T(8,128)(2,1)}, bf16[4,768,2,128]{3,2,1,0:T(2,128)(2,1)S(1)}, bf16[4,768,2,128]...) custom-call(bf16[4,1536,128]{2,1,0:T(8,128)(2,1)S(1)} %bitcast.41, ...), custom_call_target="tpu_custom_call", output_to_operand_aliasing={{0}: (3, {}), {1}: (4, {})} | custom-call | flops 5000000000 | bytes 15000000 | tf_op jit(solution)/shard_map/pallas_call | solution.py:53
  76.9 0.0 copy-start
  76.9 4.8 %shard_map.56 = (bf16[16,1536,128]{2,1,0:T(8,128)(2,1)}, bf16[16,1536,128]{2,1,0:T(8,128)(2,1)}) custom-call(bf16[4,1536,128]{2,1,0:T(8,128)(2,1)S(1)} %bitcast.49, bf16[4,1536,128]{2,1,0:T(8,128)(2,1)S(1)} %bitcast.50, bf16[4,1536,128]{2,1,0:T(8,128)(2,1)S(1)} %bitcast.51, ...), custom_call_target="tpu_custom_call", output_to_operand_aliasing={{0}: (3, {}), {1}: (4, {})} | custom-call | flops 5000000000 | bytes 15000000 | tf_op jit(solution)/shard_map/pallas_call | solution.py:53
  81.7 3.8 %all-to-all-done.1 = f32[128,32,128]{2,1,0:T(8,128)S(1)} async-done(((f32[128,32,128]{2,1,0:T(8,128)}), f32[128,32,128]{2,1,0:T(8,128)S(1)}, u32[]{:S(2)}, u32[]{:S(2)}) %all-to-all-start.1) | async-done | bytes 2097184 | tf_op jit(solution)/shard_map/all_to_all | solution.py:245
  85.6 0.0 copy-done
  85.6 3.4 %shard_map.57 = (bf16[16,256,128]{2,1,0:T(8,128)(2,1)S(1)}, bf16[16,512,128]{2,1,0:T(8,128)(2,1)S(1)}, bf16[16,512,128]{2,1,0:T(8,128)(2,1)S(1)}, bf16[32,128,128]{2,1,0:T(8,128)(2,1)S(1)}) custom-call(f32[32,128,128]{2,1,0:T(8,128)S(1)} %bitcast.30, f32[16,8,128]{2,1,0:T(8,128)S(1)} %bitcast.37, bf16[16,1536,128]{2,1,0:T(8,128)(2,1)} %get-tuple-element.75.refs_0_.refs_2_, ...), custom_call_target="tpu_custom_call" | custom-call | flops 3000000000 | bytes 9000000 | tf_op jit(solution)/shard_map/pallas_call | solution.py:53
  89.0 2.8 %shard_map.58 = (bf16[16,512,128]{2,1,0:T(8,128)(2,1)S(1)}, bf16[16,512,128]{2,1,0:T(8,128)(2,1)S(1)}, bf16[16,512,128]{2,1,0:T(8,128)(2,1)S(1)}, bf16[768,16,2,128]{3,2,1,0:T(2,128)(2,1)}) custom-call(bf16[32,128,128]{2,1,0:T(8,128)(2,1)S(1)} %get-tuple-element.77.held_ref, f32[16,8,128]{2,1,0:T(8,128)S(1)} %bitcast.38, ...), custom_call_target="tpu_custom_call" | custom-call | flops 3000000000 | bytes 9000000 | tf_op jit(solution)/shard_map/pallas_call | solution.py:53
  91.8 2.5 %shard_map.59 = (bf16[16,512,128]{2,1,0:T(8,128)(2,1)S(1)}, bf16[16,256,128]{2,1,0:T(8,128)(2,1)S(1)}, bf16[16,256,128]{2,1,0:T(8,128)(2,1)S(1)}, bf16[768,16,2,128]{3,2,1,0:T(2,128)(2,1)}) custom-call(bf16[32,128,128]{2,1,0:T(8,128)(2,1)S(1)} %get-tuple-element.77.held_ref, f32[16,8,128]{2,1,0:T(8,128)S(1)} %bitcast.39, ...), custom_call_target="tpu_custom_call", output_to_operand_aliasing={{3}: (7, {})} | custom-call | flops 3000000000 | bytes 9000000 | tf_op jit(solution)/shard_map/pallas_call | solution.py:53
  94.3 2.1 %shard_map.60 = (bf16[16,256,128]{2,1,0:T(8,128)(2,1)S(1)}, bf16[768,16,2,128]{3,2,1,0:T(2,128)(2,1)}) custom-call(bf16[32,128,128]{2,1,0:T(8,128)(2,1)S(1)} %get-tuple-element.77.held_ref, f32[16,8,128]{2,1,0:T(8,128)S(1)} %bitcast.40, bf16[16,256,128]{2,1,0:T(8,128)(2,1)S(1)} %get-tuple-element.85.refs_0_, ...), custom_call_target="tpu_custom_call", output_to_operand_aliasing={{1}: (5, {})} | custom-call | flops 3000000000 | bytes 9000000 | tf_op jit(solution)/shard_map/pallas_call | solution.py:53
  96.4 1.1 %shard_map.61 = bf16[768,16,2,128]{3,2,1,0:T(2,128)(2,1)} custom-call(bf16[16,128,2,128]{3,2,1,0:T(2,128)(2,1)S(1)} %bitcast.48, bf16[768,16,2,128]{3,2,1,0:T(2,128)(2,1)} %get-tuple-element.90._), custom_call_target="tpu_custom_call", output_to_operand_aliasing={{}: (1, {})} | custom-call | flops 1000000000 | bytes 3000000 | tf_op jit(solution)/shard_map/pallas_call | solution.py:53
  (1 shorter events, 0.0 us)
Async XLA Ops:
  50.5 35.1 %all-to-all-start.1 = ((f32[128,32,128]{2,1,0:T(8,128)}), f32[128,32,128]{2,1,0:T(8,128)S(1)}, u32[]{:S(2)}, u32[]{:S(2)}) async-start(f32[128,32,128]{2,1,0:T(8,128)} %shard_map.50), calls=%async_computation.1 | async-start | bytes 4194304 | tf_op jit(solution)/shard_map/all_to_all | solution.py:245
  76.9 8.6 %copy-start = (f32[4096]{0:T(1024)S(1)}, f32[4096]{0:T(1024)}, u32[]{:S(2)}) copy-start(f32[4096]{0:T(1024)} %param.7) | copy-start | bytes 49156
